TPU v7x, 1024 devices: a whole 4x8x16 slice. The times are simulated.
1024 devices in a mesh: dp: 8 (over y), ctx: 32 (over z_hi, x, core), tp: 4 (over z_lo).
Axes of the slice: x: 4, y: 8, z: 16 (z_hi: 4, z_lo: 4; z = z_hi * 4 + z_lo), core: 2. Of those that a mesh axis runs over, the one named last changes fastest.
Arguments:
- queries: bfloat16 [32768, 4096], P(('dp', 'ctx'), 'tp'), parts along dimension 0, may hold values from -6.5 to 6.5
- keys: bfloat16 [32768, 512], P(('dp', 'ctx'), 'tp'), parts along dimension 0, may hold values from -6.5 to 6.5
- values: bfloat16 [32768, 512], P(('dp', 'ctx'), 'tp'), parts along dimension 0, may hold values from -6 to 6
- out_weight: bfloat16 [4096, 2048], P('tp'), may hold values from -0.375 to 0.375
- norm_gain: float32 [2048], replicated, may hold values from 0.5 to 1.5
- expert_gate: bfloat16 [128, 2048, 384], P(('ctx', 'tp')), may hold values from -0.125 to 0.125
- expert_up: bfloat16 [128, 2048, 384], P(('ctx', 'tp')), may hold values from -0.125 to 0.125
- expert_down: bfloat16 [128, 384, 2048], P(('ctx', 'tp')), may hold values from -0.3125 to 0.3125
- expert_ids: int32 [32768, 8], P(('dp', 'ctx')), parts along dimension 0, may hold values from 0 to 127, as said below
- route_weights: float32 [32768, 8], P(('dp', 'ctx')), parts along dimension 0, may hold values from 0.05 to 1
Outputs:
- attended: bfloat16 [32768, 4096], P(('dp', 'ctx'), 'tp'), parts along dimension 0
- layer_out: bfloat16 [32768, 2048], P(('dp', 'ctx', 'tp')), parts along dimension 0
There are 8 independent parts, one for each index of `dp`. A program takes and returns all parts, laid end to end along the dimension named above; an argument that names none is the same for every part. Nothing has to cross between parts.
Inputs may be any that keep to these rules, and one draw needn't show every extreme that they name: `expert_ids`: each row names 8 different experts. In each aligned block of 128 rows (the rows of one ctx index) every expert is named by at least 4 and at most 12 rows, and one expert is named by exactly 12 rows in every block.
All inputs are finite; a program needn't handle non-finite values.
Results may differ from a plain program's by a relative error of at most 0.02.
Values may be sent and summed in bfloat16 or wider, within the bound.
A program may use at most 64 MiB of HBM per device.

v0:
```python
import math

import jax
import jax.numpy as jnp
from jax import lax
from jax.sharding import PartitionSpec as P

HEAD = 128


def rms_scale(proj_rows, norm_gain):
    inverse = lax.rsqrt(jnp.mean(proj_rows * proj_rows, axis=1, keepdims=True) + 1e-06)
    return (proj_rows * inverse * norm_gain).astype(jnp.bfloat16)


def per_device(
    queries,
    keys,
    values,
    out_weight,
    norm_gain,
    expert_gate,
    expert_up,
    expert_down,
    expert_ids,
    route_weights,
):
    ctx_count = lax.axis_size("ctx")
    tp_count = lax.axis_size("tp")
    ctx_index = lax.axis_index("ctx")
    tp_index = lax.axis_index("tp")
    block_rows = queries.shape[0]
    local_heads = queries.shape[1] // HEAD
    kv_local = keys.shape[1] // HEAD
    group_size = local_heads // kv_local
    query_grid = queries.reshape(block_rows, kv_local, group_size, HEAD)
    query_pos = ctx_index * block_rows + jnp.arange(block_rows, dtype=jnp.int32)
    last_query = ctx_index * block_rows + block_rows - 1
    score_scale = HEAD ** (-0.5)

    def key_step(state_now, key_part, value_part, first_key):
        running_max, row_total, accum = state_now
        key_count = key_part.shape[0]
        key_grid = key_part.reshape(key_count, kv_local, HEAD)
        value_grid = value_part.reshape(key_count, kv_local, HEAD)
        scores = (
            jnp.einsum("tkgd,ukd->kgtu", query_grid, key_grid, preferred_element_type=jnp.float32)
            * score_scale
        )
        key_pos = first_key + jnp.arange(key_count, dtype=jnp.int32)
        allowed = key_pos[None, :] <= query_pos[:, None]
        new_max = jnp.maximum(running_max, jnp.max(jnp.where(allowed, scores, -1e30), axis=3))
        key_weights = jnp.where(allowed, jnp.exp(scores - new_max[..., None]), 0.0)
        rescale = jnp.exp(running_max - new_max)
        row_total = row_total * rescale + jnp.sum(key_weights, axis=3)
        update = jnp.einsum(
            "kgtu,ukd->kgtd",
            key_weights.astype(jnp.bfloat16),
            value_grid,
            preferred_element_type=jnp.float32,
        )
        accum = accum * rescale[..., None] + update
        return (new_max, row_total, accum)

    initial = (
        jnp.full((kv_local, group_size, block_rows), -1e30, jnp.float32),
        jnp.zeros((kv_local, group_size, block_rows), jnp.float32),
        jnp.zeros((kv_local, group_size, block_rows, HEAD), jnp.float32),
    )
    running_state = initial
    key_rows = lax.all_gather(keys, "ctx", axis=0, tiled=True)
    value_rows = lax.all_gather(values, "ctx", axis=0, tiled=True)
    key_count = key_rows.shape[0]
    sub_rows = math.gcd(key_count, 512)

    def sub_step(partial_value, sub_index):
        offset = sub_index * sub_rows
        key_part = lax.dynamic_slice_in_dim(key_rows, offset, sub_rows, 0)
        value_part = lax.dynamic_slice_in_dim(value_rows, offset, sub_rows, 0)
        updated = lax.cond(
            offset <= last_query,
            lambda state_now: key_step(state_now, key_part, value_part, offset),
            lambda state_now: state_now,
            partial_value,
        )
        return (updated, None)

    running_state, unused = lax.scan(
        sub_step, running_state, jnp.arange(key_count // sub_rows, dtype=jnp.int32)
    )
    final_max, row_total, accum = running_state
    attended = (
        (accum / row_total[..., None])
        .transpose(2, 0, 1, 3)
        .reshape(block_rows, local_heads * HEAD)
        .astype(jnp.bfloat16)
    )
    share_rows = block_rows // tp_count
    partial_proj = jnp.dot(attended, out_weight, preferred_element_type=jnp.float32)
    projected = lax.psum(partial_proj.astype(jnp.bfloat16), "tp").astype(jnp.float32)
    normed = rms_scale(projected, norm_gain)
    own_proj = lax.dynamic_slice_in_dim(projected, tp_index * share_rows, share_rows, 0)
    top_count = expert_ids.shape[1]
    capacity = block_rows * top_count // (ctx_count * tp_count) * 3 // 2
    slot_total = ctx_count * capacity
    is_mine = expert_ids % tp_count == tp_index
    target_ctx = expert_ids // tp_count
    flat_target = target_ctx.reshape(-1)
    flat_mine = is_mine.reshape(-1)
    to_target = (
        flat_target[:, None] == jnp.arange(ctx_count, dtype=jnp.int32)[None, :]
    ) & flat_mine[:, None]
    running = jnp.cumsum(to_target.astype(jnp.int32), axis=0) - 1
    position = jnp.sum(jnp.where(to_target, running, 0), axis=1)
    slot_id = jnp.where(flat_mine, flat_target * capacity + position, -1).reshape(
        block_rows, top_count
    )
    slot_match = slot_id[:, :, None] == jnp.arange(slot_total, dtype=jnp.int32)[None, None, :]
    dispatch_map = jnp.any(slot_match, axis=1).astype(jnp.bfloat16)
    outgoing = jnp.einsum(
        "ts,td->sd", dispatch_map, normed, preferred_element_type=jnp.float32
    ).astype(jnp.bfloat16)
    outgoing = outgoing.reshape(ctx_count, capacity, normed.shape[1])
    route_share = route_weights / jnp.sum(route_weights, axis=1, keepdims=True)
    mix_weights = jnp.sum(jnp.where(slot_match, route_share[:, :, None], 0.0), axis=1)
    mix_high = mix_weights.astype(jnp.bfloat16)
    mix_low = (mix_weights - mix_high.astype(jnp.float32)).astype(jnp.bfloat16)
    arrived = lax.all_to_all(outgoing, "ctx", split_axis=0, concat_axis=0, tiled=True)
    source_count, item_count, features = arrived.shape
    flattened = arrived.reshape(source_count * item_count, features)
    gate_proj = jnp.dot(flattened, expert_gate[0], preferred_element_type=jnp.float32)
    up_proj = jnp.dot(flattened, expert_up[0], preferred_element_type=jnp.float32)
    activated = (jax.nn.silu(gate_proj) * up_proj).astype(jnp.bfloat16)
    expert_out = jnp.dot(activated, expert_down[0], preferred_element_type=jnp.float32).astype(
        jnp.bfloat16
    )
    expert_out = expert_out.reshape(source_count, item_count, features)
    returned = lax.all_to_all(expert_out, "ctx", split_axis=0, concat_axis=0, tiled=True)
    returned_flat = returned.reshape(slot_total, returned.shape[2])
    high_part = jnp.dot(mix_high, returned_flat, preferred_element_type=jnp.float32)
    expert_mix = lax.psum_scatter(
        (high_part + jnp.dot(mix_low, returned_flat, preferred_element_type=jnp.float32)).astype(
            jnp.bfloat16
        ),
        "tp",
        scatter_dimension=0,
        tiled=True,
    ).astype(jnp.float32)
    layer_out = (own_proj + expert_mix).astype(jnp.bfloat16)
    return (attended, layer_out)


def solution(mesh):
    in_specs = (
        P(("dp", "ctx"), "tp"),
        P(("dp", "ctx"), "tp"),
        P(("dp", "ctx"), "tp"),
        P("tp", None),
        P(),
        P(("ctx", "tp"), None, None),
        P(("ctx", "tp"), None, None),
        P(("ctx", "tp"), None, None),
        P(("dp", "ctx"), None),
        P(("dp", "ctx"), None),
    )
    out_specs = (P(("dp", "ctx"), "tp"), P(("dp", "ctx", "tp"), None))
    return jax.shard_map(
        per_device, mesh=mesh, in_specs=in_specs, out_specs=out_specs, check_vma=False
    )
```

profile of v0, /device:TPU:4, one launch (start us, length us, event | category | flops | bytes accessed | tf_op | source)
XLA Modules:
  0.0 560.2 jit_solution(1149502440124229164)
XLA Ops:
  7.2 0.7 all-gather.3.cloned.1.call-update
  7.9 0.0 all-gather.5.cloned.1.call-start
  8.0 0.7 all-gather.5.cloned.1.call-update
  8.7 0.0 all-reduce.2.cloned.1.call-start
  8.7 1.1 copy.28
  9.8 0.2 copy.29
  10.0 0.8 copy.31
  10.9 0.1 eq.52
  11.0 0.1 and.35
  11.1 9.0 %reduce-window.6 = s32[32,8,128]{2,1,0:T(8,128)S(1)} reduce-window(s32[32,8,128]{2,1,0:T(8,128)S(1)} %fusion.54, s32[]{:T(128)} %constant.93.clone.1), window={size=1x1x128 pad=0_0x0_0x127_0}, to_apply=%region_7.8 | reduce-window | flops 4161536 | bytes 262148 | tf_op jit(solution)/shard_map/reduce-window
  20.1 0.1 slice.8
  20.2 0.1 copy.35
  20.4 0.1 copy.36
  20.5 76.4 %all-gather.3.cloned.1.call-done = bf16[4096,128]{1,0:T(8,128)(2,1)} async-done(((bf16[128,128]{1,0:T(8,128)(2,1)}), bf16[4096,128]{1,0:T(8,128)(2,1)}) %all-gather.3.cloned.1.call-update) | async-done | bytes 1048592 | tf_op jit(solution)/shard_map/all_gather | solution.py:71
  96.9 76.2 %all-gather.5.cloned.1.call-done = bf16[4096,128]{1,0:T(8,128)(2,1)} async-done(((bf16[128,128]{1,0:T(8,128)(2,1)}), bf16[4096,128]{1,0:T(8,128)(2,1)}) %all-gather.5.cloned.1.call-update) | async-done | bytes 1048592 | tf_op jit(solution)/shard_map/all_gather | solution.py:72
  173.1 17.7 %while.15 = (s32[]{:T(128)}, f32[1,8,128]{2,1,0:T(8,128)S(1)}, f32[1,8,128]{2,1,0:T(8,128)S(1)}, f32[1,8,128,128]{3,2,1,0:T(8,128)S(1)}, s32[8]{0:T(128)S(1)}, /...) while((s32[]{:T(128)}, f32[1,8,128]{2,1,0:T(8,128)S(1)}, ...), condition=%wide.region_5.6_spmd.clone, body=%wide.region_0.5_spmd.clone.sunk | while | flops 274534016 | bytes 8198485 | solution.py:88
  173.1 0.6 dynamic_slice.39
  174.3 3.8 conditional.3
  174.4 0.1 broadcast_compare_fusion
  174.5 1.4 fusion.2
  175.9 0.4 fusion.6
  176.4 1.7 fusion.7
  178.1 0.6 dynamic_slice.39
  179.4 3.8 conditional.3
  179.4 0.1 broadcast_compare_fusion
  179.6 1.4 fusion.2
  180.9 0.4 fusion.6
  181.4 1.7 fusion.7
  183.2 0.6 dynamic_slice.39
  184.4 0.6 dynamic_slice.39
  185.7 0.6 dynamic_slice.39
  187.0 0.6 dynamic_slice.39
  188.2 0.6 dynamic_slice.39
  189.5 0.6 dynamic_slice.39
  190.8 0.2 fusion.49
  191.0 0.2 copy.30
  191.2 0.7 copy-done.1
  191.9 3.7 convolution_convert_fusion.2
  195.7 0.1 add_add_fusion
  195.8 0.1 eq.48
  195.9 0.1 and.32
  196.0 0.1 reduce_sum.50
  196.1 0.1 add_select_fusion.2
  196.2 0.5 fusion.31
  196.7 85.2 %all-reduce.2.cloned.1.call-done = bf16[128,2048]{1,0:T(8,128)(2,1)} async-done(((bf16[128,2048]{1,0:T(8,128)(2,1)}), bf16[128,2048]{1,0:T(8,128)(2,1)}) %all-reduce.2.cloned.1.call-update) | async-done | bytes 524304 | tf_op jit(solution)/shard_map/psum | solution.py:100
  281.9 1.2 multiply_reduce_fusion
  283.2 1.7 convolution_convert_fusion.1
  284.9 1.5 reshape.127
  286.4 109.7 %all_to_all.10 = bf16[32,12,2048]{2,1,0:T(8,128)(2,1)} all-to-all(bf16[32,12,2048]{2,1,0:T(8,128)(2,1)} %reshape.127), channel_id=1, replica_groups=mesh['dp'=8,'ctx'=32,'tp'=4] {'ctx'}, dimensions={0} | all-to-all | bytes 3145728 | tf_op jit(solution)/shard_map/all_to_all | solution.py:128
  396.2 2.5 reshape.128
  398.7 3.2 fusion.29
  401.9 4.5 convolution_convert_fusion
  406.4 3.6 reshape.129
  410.0 10.4 %all-to-all-start.1 = ((bf16[32,12,2048]{2,1,0:T(8,128)(2,1)}), bf16[32,12,2048]{2,1,0:T(8,128)(2,1)}, u32[]{:S(2)}, u32[]{:S(2)}) async-start(bf16[32,12,2048]{2,1,0:T(8,128)(2,1)} %reshape.129), calls=%async_computation.1 | async-start | bytes 4194304 | tf_op jit(solution)/shard_map/all_to_all | solution.py:138
  420.4 0.0 reduce-scatter.2.cloned.1.call-start
  420.5 0.1 copy.37
  420.6 0.5 select_reduce_fusion
  421.1 98.7 %all-to-all-done.1 = bf16[32,12,2048]{2,1,0:T(8,128)(2,1)} async-done(((bf16[32,12,2048]{2,1,0:T(8,128)(2,1)}), bf16[32,12,2048]{2,1,0:T(8,128)(2,1)}, u32[]{:S(2)}, u32[]{:S(2)}) %all-to-all-start.1) | async-done | bytes 1572896 | tf_op jit(solution)/shard_map/all_to_all | solution.py:138
  519.8 2.5 reshape.130
  522.3 0.4 fusion.58
  522.8 1.2 fusion.25
  524.0 1.1 convert_element_type.64
  525.2 26.9 %reduce-scatter.2.cloned.1.call-done = bf16[32,2048]{1,0:T(8,128)(2,1)} async-done(((bf16[128,2048]{1,0:T(8,128)(2,1)}), bf16[32,2048]{1,0:T(8,128)(2,1)}) %reduce-scatter.2.cloned.1.call-update) | async-done | bytes 131088 | tf_op jit(solution)/shard_map/reduce_scatter | solution.py:141
  552.0 1.6 add_convert_fusion
  (48 shorter events, 0.6 us)
Async XLA Ops:
  7.2 394.7 %copy-start = (bf16[1,384,2048]{2,1,0:T(8,128)(2,1)S(1)}, bf16[1,384,2048]{2,1,0:T(8,128)(2,1)}, u32[]{:S(2)}) copy-start(bf16[1,384,2048]{2,1,0:T(8,128)(2,1)} %param.21) | copy-start | bytes 4718596
  7.2 89.7 %all-gather.3.cloned.1.call-start = ((), (), s32[]{:S(2)}) async-start(), calls=%async_computation.3 | async-start | bytes 1081344 | tf_op jit(solution)/shard_map/all_gather | solution.py:71
  7.9 165.1 %all-gather.5.cloned.1.call-start = ((), (), s32[]{:S(2)}) async-start(), calls=%async_computation.4 | async-start | bytes 1081344 | tf_op jit(solution)/shard_map/all_gather | solution.py:72
  8.7 273.3 %all-reduce.2.cloned.1.call-start = ((), (), s32[]{:S(2)}) async-start(), calls=%async_computation.5 | async-start | bytes 1048576 | tf_op jit(solution)/shard_map/psum | solution.py:100
  191.2 0.7 copy-start.1
  195.7 87.5 %copy-start.3 = (f32[2048]{0:T(1024)S(1)}, f32[2048]{0:T(1024)}, u32[]{:S(2)}) copy-start(f32[2048]{0:T(1024)} %param.18) | copy-start | bytes 24580
  410.0 10.5 %copy-start.2 = (f32[128,8]{0,1:T(8,128)S(1)}, f32[128,8]{0,1:T(8,128)}, u32[]{:S(2)}) copy-start(f32[128,8]{0,1:T(8,128)} %param.23) | copy-start | bytes 12292
  410.0 109.8 %all-to-all-start.1 = ((bf16[32,12,2048]{2,1,0:T(8,128)(2,1)}), bf16[32,12,2048]{2,1,0:T(8,128)(2,1)}, u32[]{:S(2)}, u32[]{:S(2)}) async-start(bf16[32,12,2048]{2,1,0:T(8,128)(2,1)} %reshape.129), calls=%async_computation.1 | async-start | bytes 4194304 | tf_op jit(solution)/shard_map/all_to_all | solution.py:138
  420.4 131.6 %reduce-scatter.2.cloned.1.call-start = ((), (), s32[]{:S(2)}) async-start(), calls=%async_computation.6 | async-start | bytes 655360 | tf_op jit(solution)/shard_map/reduce_scatter | solution.py:141
Sparse Core Ops, SparseCore 0:
  12.3 84.5 all-gather.2
  101.2 71.8 all-gather.4
  195.8 86.0 all-reduce.1
  524.1 27.8 reduce-scatter.1
where the time goes:
time: 561 us; the launch traced here: 560 us
  waiting for transfers between devices  365 us (65%)
  blocking collectives  110 us (20%)
  matrix products  21 us (4%)
  local copies, waits for them, and re-layouts  18.8 us (3%)
  other arithmetic  15.8 us (3%)
  between operations  14 us (2%)
  starting transfers between devices  10.6 us (2%)
    all_to_all x1, blocking collectives, per_device(): lax.all_to_all(outgoing, 'ctx', split_axis=0, concat_axis=0, tiled=True)  110 us
    all_to_all x1, waiting for transfers between devices, per_device(): lax.all_to_all(expert_out, 'ctx', split_axis=0, concat_axis=0, tiled=True)  98.7 us
    psum x1, waiting for transfers between devices, per_device(): lax.psum(partial_proj.astype(jnp.bfloat16), 'tp').astype(jnp.float32)  85.2 us
    all_gather x1, waiting for transfers between devices, per_device(): key_rows = lax.all_gather(keys, 'ctx', axis=0, tiled=True)  76.4 us
    all_gather x1, waiting for transfers between devices, per_device(): value_rows = lax.all_gather(values, 'ctx', axis=0, tiled=True)  76.2 us
    reduce_scatter x1, waiting for transfers between devices, per_device(): lax.psum_scatter((high_part + jnp.dot(mix_low, returned_flat, preferred_e...  26.9 us
  transfers between devices with their start and end apart: 5, of which 5 were waited for; matrix products, arithmetic and copies ran while one was open for 3% of the time, Pallas kernels for 0%

commit v1 on v0

v1 whole, which is shorter than its diff:
```python
import math

import jax
import jax.numpy as jnp
from jax import lax
from jax.experimental import pallas as pl
from jax.experimental.pallas import tpu as pltpu
from jax.sharding import PartitionSpec as P

MESH = pl.DeviceIdType.MESH
BF16 = jnp.bfloat16
F32 = jnp.float32
HEAD = 128
HEADS = 8
BLK = 128
D = 2048
EFF = 384
ROWS = 32
SLOTS = 16
NEG = -1e30


def layer_kernel(
    q_hbm, k_hbm, v_hbm, w_hbm, gain_hbm, gate_hbm, up_hbm, down_hbm, route_hbm,
    att_hbm, out_hbm,
    q_v, q_h, kv, w_v, gain_v, gate_v, up_v, down_v, route,
    m_s, l_s, acc_s, att_v, proj_f, rs_s, rs_r, proj_own,
    dmap, mmap, xg, xs, xr, ys, ret, contrib, sp, sm, rp, rm, out_v,
    load_sem, send_sem, kv_sem, route_sem, rs_sem, agp_sem, agm_sem, xd_sem, xb_sem, rp_sem, rm_sem, self_sem,
):
    ctx = lax.axis_index("ctx")
    tp = lax.axis_index("tp")
    zh = ctx // 8
    row = ctx % 8
    x = row // 2
    core = ctx % 2
    z = zh * 4 + tp

    sends = []

    def send(src, dst, recv_sem, device):
        copy = pltpu.make_async_remote_copy(
            src_ref=src, dst_ref=dst, send_sem=send_sem.at[len(sends)], recv_sem=recv_sem,
            device_id=device, device_id_type=MESH,
        )
        copy.start()
        sends.append(copy)

    def arrived(dst, recv_sem):
        pltpu.make_async_remote_copy(
            src_ref=dst, dst_ref=dst, send_sem=send_sem.at[0], recv_sem=recv_sem,
            device_id=at_row(row), device_id_type=MESH,
        ).wait_recv()

    def at_zh(z_hi):
        return {"ctx": z_hi * 8 + row, "tp": tp}

    def at_row(r):
        return {"ctx": zh * 8 + r, "tp": tp}

    def at_z(zz):
        return {"ctx": (zz // 4) * 8 + row, "tp": zz % 4}

    def at_tp(t):
        return {"ctx": ctx, "tp": t}

    def zmod(offset):
        return (z + offset + 16) % 16

    loads = {}

    def load(name, src, dst):
        copy = pltpu.make_async_copy(src, dst, load_sem.at[len(loads)])
        copy.start()
        loads[name] = copy

    load("k", k_hbm, kv.at[ctx, pl.ds(0, BLK)])
    load("v", v_hbm, kv.at[ctx, pl.ds(BLK, BLK)])
    load("route", route_hbm, route.at[zh])
    load("q", q_hbm, q_v)
    load("w", w_hbm, w_v)
    load("gain", gain_hbm, gain_v)
    load("gate", gate_hbm, gate_v)
    load("up", up_hbm, up_v)
    load("down", down_hbm, down_v)

    barrier = pltpu.get_barrier_semaphore()
    partners = [at_zh((zh + d) % 4) for d in (1, 2, 3)]
    partners += [at_row((row + o) % 8) for o in range(1, 8)]
    partners += [at_tp((tp + o) % 4) for o in (1, 2, 3)]
    partners += [at_z(zmod(1)), at_z(zmod(-1))]
    for partner in partners:
        pl.semaphore_signal(barrier, inc=1, device_id=partner, device_id_type=MESH)
    pl.semaphore_wait(barrier, len(partners))

    sibling = row + 1 - 2 * core
    loads["k"].wait()
    loads["v"].wait()

    def send_block(block, device):
        send(kv.at[block], kv.at[block], kv_sem.at[block], device)

    def x_row(dx):
        return ((x + dx) % 4) * 2 + core

    for d in (2, 1, 3):
        send_block(ctx, at_zh((zh + d) % 4))
    for dx in (2, 1, 3):
        send_block(ctx, at_row(x_row(dx)))
    send_block(ctx, at_row(sibling))
    loads["route"].wait()
    for d in (1, 2, 3):
        send(route.at[zh], route.at[zh], route_sem.at[zh], at_zh((zh + d) % 4))

    loads["q"].wait()
    for h in range(HEADS):
        q_h[h] = q_v[:, h * HEAD : (h + 1) * HEAD]

    score_scale = (HEAD**-0.5) * math.log2(math.e)

    def attend(s, first):
        def head(h, carry):
            keys = kv[pl.ds(s * 8, 8), 0:BLK, :].reshape(8 * BLK, HEAD)
            vals = kv[pl.ds(s * 8, 8), BLK : 2 * BLK, :].reshape(8 * BLK, HEAD)
            scores = lax.dot_general(
                q_h[h], keys, (((1,), (1,)), ((), ())), preferred_element_type=F32
            )
            scores = scores * score_scale
            if first:
                key_pos = lax.broadcasted_iota(jnp.int32, scores.shape, 1)
                query_pos = lax.broadcasted_iota(jnp.int32, scores.shape, 0) + row * BLK
                scores = jnp.where(key_pos <= query_pos, scores, NEG)
            top = jnp.max(scores, axis=1, keepdims=True)
            if first:
                new_max = jnp.broadcast_to(top, (BLK, HEAD))
            else:
                new_max = jnp.maximum(m_s[h], top)
            weights = [
                jnp.exp2(scores[:, j * HEAD : (j + 1) * HEAD] - new_max) for j in range(8)
            ]
            total = weights[0]
            for j in range(1, 8):
                total = total + weights[j]
            update = jnp.dot(
                jnp.concatenate([w.astype(BF16) for w in weights], axis=1),
                vals,
                preferred_element_type=F32,
            )
            if first:
                l_s[h] = total
                acc_s[h] = update
            else:
                rescale = jnp.exp2(m_s[h] - new_max)
                l_s[h] = l_s[h] * rescale + total
                acc_s[h] = acc_s[h] * rescale + update
            m_s[h] = new_max
            return carry

        lax.fori_loop(0, HEADS, head, 0)

    def collect(s):
        for dx in (1, 3, 2):
            block = s * 8 + x_row(dx)
            arrived(kv.at[block], kv_sem.at[block])
            send_block(block, at_row(sibling))
        for dx in (0, 1, 3, 2):
            block = s * 8 + ((x + dx) % 4) * 2 + 1 - core
            arrived(kv.at[block], kv_sem.at[block])

    collect(zh)
    attend(zh, True)

    for d in (1, 3, 2):
        block = ((zh + d) % 4) * 8 + row
        arrived(kv.at[block], kv_sem.at[block])
        for dx in (2, 1, 3):
            send_block(block, at_row(x_row(dx)))
        send_block(block, at_row(sibling))

    for d in (1, 2, 3):
        src = (zh + d) % 4
        arrived(route.at[src], route_sem.at[src])
    earlier = (
        lax.broadcasted_iota(jnp.int32, (BLK, BLK), 0)
        < lax.broadcasted_iota(jnp.int32, (BLK, BLK), 1)
    ).astype(F32).astype(BF16)
    slot = lax.broadcasted_iota(jnp.int32, (SLOTS, BLK), 0).astype(F32)
    for b in range(4):
        ids = route[b, 0:8, :]
        share = route[b, 8:16, :]
        share = share / jnp.sum(share, axis=0, keepdims=True)
        hits, picked = [], []
        for r in range(8):
            same = ids == (zh * 32 + tp + 4 * r).astype(F32)
            hits.append(jnp.sum(jnp.where(same, 1.0, 0.0), axis=0, keepdims=True))
            picked.append(jnp.sum(jnp.where(same, share, 0.0), axis=0, keepdims=True))
        hit = jnp.concatenate(hits, axis=0)
        rank = jnp.dot(hit.astype(BF16), earlier, preferred_element_type=F32)
        choose = [
            jnp.where(slot == rank[r : r + 1], hit[r : r + 1], 0.0) for r in range(8)
        ]
        dmap[b] = jnp.concatenate(choose, axis=0).astype(BF16)
        back = jnp.concatenate([choose[r] * picked[r] for r in range(8)], axis=0)
        mmap[b] = back.T.astype(BF16)

    for d in (3, 1, 2):
        s = (zh + d) % 4
        collect(s)

        @pl.when(s < zh)
        def _():
            attend(s, False)

    for h in range(HEADS):
        att_v[:, h * HEAD : (h + 1) * HEAD] = (
            acc_s[h] / jnp.sum(l_s[h], axis=1, keepdims=True)
        ).astype(BF16)
    att_store = pltpu.make_async_copy(att_v, att_hbm, self_sem.at[8])
    att_store.start()

    loads["w"].wait()
    for half in range(2):
        for n in range(2):
            cols = pl.ds(half * 1024 + n * 512, 512)
            part = jnp.dot(att_v[...], w_v[:, cols], preferred_element_type=F32)
            proj_f[:, cols] = part
            rs_s[:, cols] = part.astype(BF16)
        cols = pl.ds(half * 1024, 1024)
        for o in (2, 1, 3):
            owner = (tp + o) % 4
            send(
                rs_s.at[pl.ds(pl.multiple_of(owner * ROWS, ROWS), ROWS), cols],
                rs_r.at[o - 1, :, cols],
                rs_sem.at[half, o - 1],
                at_tp(owner),
            )
    loads["gain"].wait()
    for half in range(2):
        cols = pl.ds(half * 1024, 1024)
        for o in (2, 1, 3):
            arrived(rs_r.at[o - 1, :, cols], rs_sem.at[half, o - 1])
    own_rows = pl.ds(pl.multiple_of(tp * ROWS, ROWS), ROWS)
    projected = (
        proj_f[own_rows, :] + rs_r[0].astype(F32) + rs_r[1].astype(F32) + rs_r[2].astype(F32)
    )
    proj_own[...] = projected
    inverse = lax.rsqrt(jnp.mean(projected * projected, axis=1, keepdims=True) + 1e-06)
    xg[zh, own_rows, :] = (projected * inverse * gain_v[...]).astype(BF16)

    def piece(origin, half):
        start = pl.multiple_of((origin % 4) * ROWS + half * 16, 16)
        return xg.at[origin // 4, pl.ds(start, 16)]

    def ring_step(k):
        for half in range(2):
            if k > 1:
                arrived(piece(zmod(1 - k), half), agp_sem.at[half, k - 2])
            here = piece(zmod(1 - k), half)
            send(here, here, agp_sem.at[half, k - 1], at_z(zmod(1)))
            if k > 1:
                arrived(piece(zmod(k - 1), half), agm_sem.at[half, k - 2])
            if k <= 7:
                here = piece(zmod(k - 1), half)
                send(here, here, agm_sem.at[half, k - 1], at_z(zmod(-1)))

    def ring_end():
        for half in range(2):
            arrived(piece(zmod(-8), half), agp_sem.at[half, 7])

    side = 2 * (tp // 2) - 1
    order = [zh, (zh + side + 4) % 4, (zh - side + 4) % 4, (zh + 2) % 4]
    own_slots = pl.ds(pl.multiple_of(row * SLOTS, SLOTS), SLOTS)
    local = {}

    def exchange(src, dst, sems, i, n):
        for o in (4, 5, 3, 2, 6, 7, 1):
            r = (row + o) % 8
            slots = pl.ds(pl.multiple_of(r * SLOTS, SLOTS), SLOTS)
            send(src.at[i, slots], dst.at[i, own_slots], sems.at[i, o], at_row(r))
        copy = pltpu.make_async_copy(
            src.at[i, own_slots], dst.at[i, own_slots], self_sem.at[n]
        )
        copy.start()
        local[n] = copy

    def exchanged(dst, sems, i, copy):
        for o in range(1, 8):
            r = (row - o + 8) % 8
            slots = pl.ds(pl.multiple_of(r * SLOTS, SLOTS), SLOTS)
            arrived(dst.at[i, slots], sems.at[i, o])
        copy.wait()

    def dispatch(i):
        for n in range(4):
            cols = pl.ds(n * 512, 512)
            xs[i, :, cols] = jnp.dot(
                dmap[order[i]], xg[order[i], :, cols], preferred_element_type=F32
            ).astype(BF16)
        exchange(xs, xr, xd_sem, i, i)

    def expert(i):
        exchanged(xr, xd_sem, i, local[i])
        items = xr[i]
        gate = jnp.dot(items, gate_v[...], preferred_element_type=F32)
        up = jnp.dot(items, up_v[...], preferred_element_type=F32)
        act = (gate / (1.0 + jnp.exp(-gate)) * up).astype(BF16)
        for n in range(4):
            cols = pl.ds(n * 512, 512)
            ys[i, :, cols] = jnp.dot(
                act, down_v[:, cols], preferred_element_type=F32
            ).astype(BF16)
        exchange(ys, ret, xb_sem, i, 4 + i)

    def mix(i):
        exchanged(ret, xb_sem, i, local[4 + i])
        for n in range(4):
            cols = pl.ds(n * 512, 512)
            contrib[order[i], :, cols] = jnp.dot(
                mmap[order[i]], ret[i, :, cols], preferred_element_type=F32
            )

    for k in (1, 2, 3, 4):
        ring_step(k)
    dispatch(0)
    for k in (5, 6):
        ring_step(k)
    dispatch(1)
    for k in (7, 8):
        ring_step(k)
    dispatch(2)
    loads["gate"].wait()
    loads["up"].wait()
    loads["down"].wait()
    expert(0)
    ring_end()
    dispatch(3)
    expert(1)
    expert(2)
    expert(3)
    mix(0)
    mix(1)
    mix(2)
    mix(3)

    def term(dest, half):
        start = pl.multiple_of((dest % 4) * ROWS + half * 16, 16)
        return contrib[dest // 4, pl.ds(start, 16), :]

    for k in range(1, 9):
        for half in range(2):
            rows = pl.ds(half * 16, 16)
            total = term(zmod(9 - k), half)
            if k > 1:
                arrived(rp.at[k - 2, rows], rp_sem.at[half, k - 2])
                total = total + rp[k - 2, rows].astype(F32)
            sp[k - 1, rows] = total.astype(BF16)
            send(sp.at[k - 1, rows], rp.at[k - 1, rows], rp_sem.at[half, k - 1], at_z(zmod(1)))
            if k <= 7:
                total = term(zmod(k - 8), half)
                if k > 1:
                    arrived(rm.at[k - 2, rows], rm_sem.at[half, k - 2])
                    total = total + rm[k - 2, rows].astype(F32)
                sm[k - 1, rows] = total.astype(BF16)
                send(
                    sm.at[k - 1, rows], rm.at[k - 1, rows], rm_sem.at[half, k - 1], at_z(zmod(-1))
                )
    for half in range(2):
        rows = pl.ds(half * 16, 16)
        arrived(rm.at[6, rows], rm_sem.at[half, 6])
        arrived(rp.at[7, rows], rp_sem.at[half, 7])
        out_v[rows] = (
            proj_own[rows]
            + term(z, half)
            + rp[7, rows].astype(F32)
            + rm[6, rows].astype(F32)
        ).astype(BF16)
    out_store = pltpu.make_async_copy(out_v, out_hbm, self_sem.at[9])
    out_store.start()
    for copy in sends:
        copy.wait_send()
    att_store.wait()
    out_store.wait()


def per_device(
    queries, keys, values, out_weight, norm_gain,
    expert_gate, expert_up, expert_down, expert_ids, route_weights,
):
    route = jnp.concatenate([expert_ids.astype(F32), route_weights], axis=1).T
    any_spec = pl.BlockSpec(memory_space=pl.ANY)
    vmem = pltpu.VMEM
    dma = pltpu.SemaphoreType.DMA
    return pl.pallas_call(
        layer_kernel,
        out_shape=(
            jax.ShapeDtypeStruct((BLK, HEADS * HEAD), BF16),
            jax.ShapeDtypeStruct((ROWS, D), BF16),
        ),
        in_specs=[any_spec] * 9,
        out_specs=(any_spec, any_spec),
        scratch_shapes=[
            vmem((BLK, HEADS * HEAD), BF16),
            vmem((HEADS, BLK, HEAD), BF16),
            vmem((32, 2 * BLK, HEAD), BF16),
            vmem((HEADS * HEAD, D), BF16),
            vmem((1, D), F32),
            vmem((D, EFF), BF16),
            vmem((D, EFF), BF16),
            vmem((EFF, D), BF16),
            vmem((4, 16, BLK), F32),
            vmem((HEADS, BLK, HEAD), F32),
            vmem((HEADS, BLK, HEAD), F32),
            vmem((HEADS, BLK, HEAD), F32),
            vmem((BLK, HEADS * HEAD), BF16),
            vmem((BLK, D), F32),
            vmem((BLK, D), BF16),
            vmem((3, ROWS, D), BF16),
            vmem((ROWS, D), F32),
            vmem((4, 8 * SLOTS, BLK), BF16),
            vmem((4, BLK, 8 * SLOTS), BF16),
            vmem((4, BLK, D), BF16),
            vmem((4, 8 * SLOTS, D), BF16),
            vmem((4, 8 * SLOTS, D), BF16),
            vmem((4, 8 * SLOTS, D), BF16),
            vmem((4, 8 * SLOTS, D), BF16),
            vmem((4, BLK, D), F32),
            vmem((8, ROWS, D), BF16),
            vmem((7, ROWS, D), BF16),
            vmem((8, ROWS, D), BF16),
            vmem((7, ROWS, D), BF16),
            vmem((ROWS, D), BF16),
            dma((9,)),
            dma((180,)),
            dma((32,)),
            dma((4,)),
            dma((2, 3)),
            dma((2, 8)),
            dma((2, 7)),
            dma((4, 8)),
            dma((4, 8)),
            dma((2, 8)),
            dma((2, 7)),
            dma((10,)),
        ],
        compiler_params=pltpu.CompilerParams(
            collective_id=0, has_side_effects=True, vmem_limit_bytes=60 * 1024 * 1024
        ),
        name="layer",
    )(
        queries, keys, values, out_weight, norm_gain.reshape(1, D),
        expert_gate.reshape(D, EFF), expert_up.reshape(D, EFF), expert_down.reshape(EFF, D), route,
    )


def solution(mesh):
    in_specs = (
        P(("dp", "ctx"), "tp"),
        P(("dp", "ctx"), "tp"),
        P(("dp", "ctx"), "tp"),
        P("tp", None),
        P(),
        P(("ctx", "tp"), None, None),
        P(("ctx", "tp"), None, None),
        P(("ctx", "tp"), None, None),
        P(("dp", "ctx"), None),
        P(("dp", "ctx"), None),
    )
    out_specs = (P(("dp", "ctx"), "tp"), P(("dp", "ctx", "tp"), None))
    return jax.shard_map(
        per_device, mesh=mesh, in_specs=in_specs, out_specs=out_specs, check_vma=False
    )
```

time: 561 us -> 171 us (0.30)
  the two profiles are of different devices: /device:TPU:4 before, /device:TPU:48 now
where the time goes in v1:
time: 171 us
  Pallas kernels  165 us (96%)
  local copies, waits for them, and re-layouts  3.24 us (2%)
  other arithmetic  1.98 us (1%)
    pallas_call x1, Pallas kernels, per_device(): pl.pallas_call(layer_kernel, out_shape=(jax.ShapeDtypeStruct((BLK, HEADS...  165 us

profile of v1, /device:TPU:48, one launch (start us, length us, event | category | flops | bytes accessed | tf_op | source)
XLA Modules:
  0.0 171.0 jit_solution(16510921112461083758)
XLA Ops:
  0.6 0.7 convert_element_type.3
  1.3 1.3 maximum_bitcast_fusion.route_hbm
  2.6 165.2 %layer.1 = (bf16[128,1024]{1,0:T(8,128)(2,1)}, bf16[32,2048]{1,0:T(8,128)(2,1)}) custom-call(bf16[128,1024]{1,0:T(8,128)(2,1)} %q_hbm.1, bf16[128,128]{1,0:T(8,128)(2,1)} %k_hbm.1, bf16[128,128]{1,0:T(8,128)(2,1)} %v_hbm.1, bf16[1024,2048]{1,0:T(8,128)(2,1)} %w_hbm.1, f32[1,2048]{1,0:T(1,128)} %bitcast.9, bf16[2048,384]{1,0:T(8,128)(2,1)} %bitcast.6, ...), custom_call_target="tpu_custom_call" | custom-call | tf_op jit(solution)/shard_map/layer/pallas_call | solution.py:393
  167.8 1.7 copy.14
  169.5 1.6 copy.15

commit v2 on v1

--- a/solution.py
+++ b/solution.py
@@ -21,9 +21,9 @@
 
 
 def layer_kernel(
-    q_hbm, k_hbm, v_hbm, w_hbm, gain_hbm, gate_hbm, up_hbm, down_hbm, route_hbm,
+    q_hbm, k_hbm, v_hbm, w_hbm, gain_hbm, gate_hbm, up_hbm, down_hbm, ids_hbm, share_hbm,
     att_hbm, out_hbm,
-    q_v, q_h, kv, w_v, gain_v, gate_v, up_v, down_v, route,
+    q_v, q_h, kv, w_v, gain_v, gate_v, up_v, down_v, ids_v, share_v, route,
     m_s, l_s, acc_s, att_v, proj_f, rs_s, rs_r, proj_own,
     dmap, mmap, xg, xs, xr, ys, ret, contrib, sp, sm, rp, rm, out_v,
     load_sem, send_sem, kv_sem, route_sem, rs_sem, agp_sem, agm_sem, xd_sem, xb_sem, rp_sem, rm_sem, self_sem,
@@ -76,7 +76,8 @@
 
     load("k", k_hbm, kv.at[ctx, pl.ds(0, BLK)])
     load("v", v_hbm, kv.at[ctx, pl.ds(BLK, BLK)])
-    load("route", route_hbm, route.at[zh])
+    load("ids", ids_hbm, ids_v)
+    load("share", share_hbm, share_v)
     load("q", q_hbm, q_v)
     load("w", w_hbm, w_v)
     load("gain", gain_hbm, gain_v)
@@ -85,12 +86,22 @@
     load("down", down_hbm, down_v)
 
     barrier = pltpu.get_barrier_semaphore()
-    partners = [at_zh((zh + d) % 4) for d in (1, 2, 3)]
+    partners = [at_zh((zh + d) % 4) for d in (1, 3)]
     partners += [at_row((row + o) % 8) for o in range(1, 8)]
     partners += [at_tp((tp + o) % 4) for o in (1, 2, 3)]
-    partners += [at_z(zmod(1)), at_z(zmod(-1))]
+    above, below = at_z(zmod(1)), at_z(zmod(-1))
+    partners += [above, below]
     for partner in partners:
         pl.semaphore_signal(barrier, inc=1, device_id=partner, device_id_type=MESH)
+
+    loads["ids"].wait()
+    loads["share"].wait()
+    route[zh, 0:8, :] = ids_v[...].astype(F32)
+    route[zh, 8:16, :] = share_v[...]
+    loads["q"].wait()
+    for h in range(HEADS):
+        q_h[h] = q_v[:, h * HEAD : (h + 1) * HEAD]
+
     pl.semaphore_wait(barrier, len(partners))
 
     sibling = row + 1 - 2 * core
@@ -103,18 +114,13 @@
     def x_row(dx):
         return ((x + dx) % 4) * 2 + core
 
-    for d in (2, 1, 3):
+    for d in (1, 3):
         send_block(ctx, at_zh((zh + d) % 4))
     for dx in (2, 1, 3):
         send_block(ctx, at_row(x_row(dx)))
     send_block(ctx, at_row(sibling))
-    loads["route"].wait()
-    for d in (1, 2, 3):
+    for d in (1, 3):
         send(route.at[zh], route.at[zh], route_sem.at[zh], at_zh((zh + d) % 4))
-
-    loads["q"].wait()
-    for h in range(HEADS):
-        q_h[h] = q_v[:, h * HEAD : (h + 1) * HEAD]
 
     score_scale = (HEAD**-0.5) * math.log2(math.e)
 
@@ -170,16 +176,39 @@
     collect(zh)
     attend(zh, True)
 
-    for d in (1, 3, 2):
-        block = ((zh + d) % 4) * 8 + row
-        arrived(kv.at[block], kv_sem.at[block])
+    def spread(block):
         for dx in (2, 1, 3):
             send_block(block, at_row(x_row(dx)))
         send_block(block, at_row(sibling))
 
-    for d in (1, 2, 3):
+    for d in (3, 1):
+        block = ((zh + d) % 4) * 8 + row
+        arrived(kv.at[block], kv_sem.at[block])
+    send_block(((zh + 3 + 2 * core) % 4) * 8 + row, at_zh((zh + 1 + 2 * core) % 4))
+    for d in (3, 1):
+        spread(((zh + d) % 4) * 8 + row)
+    for d in (3, 1):
         src = (zh + d) % 4
         arrived(route.at[src], route_sem.at[src])
+    src = (zh + 3) % 4
+    send(route.at[src], route.at[src], route_sem.at[src], at_zh((zh + 1) % 4))
+
+    def attend_earlier(d):
+        s = (zh + d) % 4
+        collect(s)
+
+        @pl.when(s < zh)
+        def _():
+            attend(s, False)
+
+    attend_earlier(3)
+    block = ((zh + 2) % 4) * 8 + row
+    arrived(kv.at[block], kv_sem.at[block])
+    spread(block)
+    attend_earlier(1)
+
+    src = (zh + 2) % 4
+    arrived(route.at[src], route_sem.at[src])
     earlier = (
         lax.broadcasted_iota(jnp.int32, (BLK, BLK), 0)
         < lax.broadcasted_iota(jnp.int32, (BLK, BLK), 1)
@@ -203,13 +232,7 @@
         back = jnp.concatenate([choose[r] * picked[r] for r in range(8)], axis=0)
         mmap[b] = back.T.astype(BF16)
 
-    for d in (3, 1, 2):
-        s = (zh + d) % 4
-        collect(s)
-
-        @pl.when(s < zh)
-        def _():
-            attend(s, False)
+    attend_earlier(2)
 
     for h in range(HEADS):
         att_v[:, h * HEAD : (h + 1) * HEAD] = (
@@ -219,53 +242,50 @@
     att_store.start()
 
     loads["w"].wait()
-    for half in range(2):
-        for n in range(2):
-            cols = pl.ds(half * 1024 + n * 512, 512)
-            part = jnp.dot(att_v[...], w_v[:, cols], preferred_element_type=F32)
-            proj_f[:, cols] = part
-            rs_s[:, cols] = part.astype(BF16)
-        cols = pl.ds(half * 1024, 1024)
+    for n in range(4):
+        cols = pl.ds(n * 512, 512)
+        part = jnp.dot(att_v[...], w_v[:, cols], preferred_element_type=F32)
+        proj_f[:, cols] = part
+        rs_s[:, cols] = part.astype(BF16)
         for o in (2, 1, 3):
             owner = (tp + o) % 4
             send(
                 rs_s.at[pl.ds(pl.multiple_of(owner * ROWS, ROWS), ROWS), cols],
                 rs_r.at[o - 1, :, cols],
-                rs_sem.at[half, o - 1],
+                rs_sem.at[n, o - 1],
                 at_tp(owner),
             )
     loads["gain"].wait()
-    for half in range(2):
-        cols = pl.ds(half * 1024, 1024)
+    for n in range(4):
+        cols = pl.ds(n * 512, 512)
         for o in (2, 1, 3):
-            arrived(rs_r.at[o - 1, :, cols], rs_sem.at[half, o - 1])
+            arrived(rs_r.at[o - 1, :, cols], rs_sem.at[n, o - 1])
     own_rows = pl.ds(pl.multiple_of(tp * ROWS, ROWS), ROWS)
     projected = (
         proj_f[own_rows, :] + rs_r[0].astype(F32) + rs_r[1].astype(F32) + rs_r[2].astype(F32)
     )
     proj_own[...] = projected
     inverse = lax.rsqrt(jnp.mean(projected * projected, axis=1, keepdims=True) + 1e-06)
-    xg[zh, own_rows, :] = (projected * inverse * gain_v[...]).astype(BF16)
-
-    def piece(origin, half):
-        start = pl.multiple_of((origin % 4) * ROWS + half * 16, 16)
-        return xg.at[origin // 4, pl.ds(start, 16)]
+    xg[z] = (projected * inverse * gain_v[...]).astype(BF16)
+
+    def piece(origin, n):
+        return xg.at[origin, :, pl.ds(n * 512, 512)]
 
     def ring_step(k):
-        for half in range(2):
+        for n in range(4):
+            here = piece(zmod(1 - k), n)
             if k > 1:
-                arrived(piece(zmod(1 - k), half), agp_sem.at[half, k - 2])
-            here = piece(zmod(1 - k), half)
-            send(here, here, agp_sem.at[half, k - 1], at_z(zmod(1)))
+                arrived(here, agp_sem.at[n, k - 2])
+            send(here, here, agp_sem.at[n, k - 1], above)
+            here = piece(zmod(k - 1), n)
             if k > 1:
-                arrived(piece(zmod(k - 1), half), agm_sem.at[half, k - 2])
+                arrived(here, agm_sem.at[n, k - 2])
             if k <= 7:
-                here = piece(zmod(k - 1), half)
-                send(here, here, agm_sem.at[half, k - 1], at_z(zmod(-1)))
+                send(here, here, agm_sem.at[n, k - 1], below)
 
     def ring_end():
-        for half in range(2):
-            arrived(piece(zmod(-8), half), agp_sem.at[half, 7])
+        for n in range(4):
+            arrived(piece(zmod(-8), n), agp_sem.at[n, 7])
 
     side = 2 * (tp // 2) - 1
     order = [zh, (zh + side + 4) % 4, (zh - side + 4) % 4, (zh + 2) % 4]
@@ -294,7 +314,9 @@
         for n in range(4):
             cols = pl.ds(n * 512, 512)
             xs[i, :, cols] = jnp.dot(
-                dmap[order[i]], xg[order[i], :, cols], preferred_element_type=F32
+                dmap[order[i]],
+                xg[pl.ds(order[i] * 4, 4), :, cols].reshape(BLK, 512),
+                preferred_element_type=F32,
             ).astype(BF16)
         exchange(xs, xr, xd_sem, i, i)
 
@@ -315,9 +337,9 @@
         exchanged(ret, xb_sem, i, local[4 + i])
         for n in range(4):
             cols = pl.ds(n * 512, 512)
-            contrib[order[i], :, cols] = jnp.dot(
+            contrib[pl.ds(order[i] * 4, 4), :, cols] = jnp.dot(
                 mmap[order[i]], ret[i, :, cols], preferred_element_type=F32
-            )
+            ).reshape(4, ROWS, 512)
 
     for k in (1, 2, 3, 4):
         ring_step(k)
@@ -325,54 +347,48 @@
     for k in (5, 6):
         ring_step(k)
     dispatch(1)
-    for k in (7, 8):
-        ring_step(k)
-    dispatch(2)
+    ring_step(7)
     loads["gate"].wait()
     loads["up"].wait()
     loads["down"].wait()
     expert(0)
+    ring_step(8)
+    dispatch(2)
+    expert(1)
     ring_end()
     dispatch(3)
-    expert(1)
     expert(2)
-    expert(3)
     mix(0)
     mix(1)
+    expert(3)
     mix(2)
     mix(3)
 
-    def term(dest, half):
-        start = pl.multiple_of((dest % 4) * ROWS + half * 16, 16)
-        return contrib[dest // 4, pl.ds(start, 16), :]
-
     for k in range(1, 9):
-        for half in range(2):
-            rows = pl.ds(half * 16, 16)
-            total = term(zmod(9 - k), half)
+        for n in range(4):
+            cols = pl.ds(n * 512, 512)
+            total = contrib[zmod(9 - k), :, cols]
             if k > 1:
-                arrived(rp.at[k - 2, rows], rp_sem.at[half, k - 2])
-                total = total + rp[k - 2, rows].astype(F32)
-            sp[k - 1, rows] = total.astype(BF16)
-            send(sp.at[k - 1, rows], rp.at[k - 1, rows], rp_sem.at[half, k - 1], at_z(zmod(1)))
+                arrived(rp.at[k - 2, :, cols], rp_sem.at[n, k - 2])
+                total = total + rp[k - 2, :, cols].astype(F32)
+            sp[k - 1, :, cols] = total.astype(BF16)
+            send(sp.at[k - 1, :, cols], rp.at[k - 1, :, cols], rp_sem.at[n, k - 1], above)
             if k <= 7:
-                total = term(zmod(k - 8), half)
+                total = contrib[zmod(k - 8), :, cols]
                 if k > 1:
-                    arrived(rm.at[k - 2, rows], rm_sem.at[half, k - 2])
-                    total = total + rm[k - 2, rows].astype(F32)
-                sm[k - 1, rows] = total.astype(BF16)
-                send(
-                    sm.at[k - 1, rows], rm.at[k - 1, rows], rm_sem.at[half, k - 1], at_z(zmod(-1))
-                )
-    for half in range(2):
-        rows = pl.ds(half * 16, 16)
-        arrived(rm.at[6, rows], rm_sem.at[half, 6])
-        arrived(rp.at[7, rows], rp_sem.at[half, 7])
-        out_v[rows] = (
-            proj_own[rows]
-            + term(z, half)
-            + rp[7, rows].astype(F32)
-            + rm[6, rows].astype(F32)
+                    arrived(rm.at[k - 2, :, cols], rm_sem.at[n, k - 2])
+                    total = total + rm[k - 2, :, cols].astype(F32)
+                sm[k - 1, :, cols] = total.astype(BF16)
+                send(sm.at[k - 1, :, cols], rm.at[k - 1, :, cols], rm_sem.at[n, k - 1], below)
+    for n in range(4):
+        cols = pl.ds(n * 512, 512)
+        arrived(rm.at[6, :, cols], rm_sem.at[n, 6])
+        arrived(rp.at[7, :, cols], rp_sem.at[n, 7])
+        out_v[:, cols] = (
+            proj_own[:, cols]
+            + contrib[z, :, cols]
+            + rp[7, :, cols].astype(F32)
+            + rm[6, :, cols].astype(F32)
         ).astype(BF16)
     out_store = pltpu.make_async_copy(out_v, out_hbm, self_sem.at[9])
     out_store.start()
@@ -386,7 +402,6 @@
     queries, keys, values, out_weight, norm_gain,
     expert_gate, expert_up, expert_down, expert_ids, route_weights,
 ):
-    route = jnp.concatenate([expert_ids.astype(F32), route_weights], axis=1).T
     any_spec = pl.BlockSpec(memory_space=pl.ANY)
     vmem = pltpu.VMEM
     dma = pltpu.SemaphoreType.DMA
@@ -396,7 +411,7 @@
             jax.ShapeDtypeStruct((BLK, HEADS * HEAD), BF16),
             jax.ShapeDtypeStruct((ROWS, D), BF16),
         ),
-        in_specs=[any_spec] * 9,
+        in_specs=[any_spec] * 10,
         out_specs=(any_spec, any_spec),
         scratch_shapes=[
             vmem((BLK, HEADS * HEAD), BF16),
@@ -407,6 +422,8 @@
             vmem((D, EFF), BF16),
             vmem((D, EFF), BF16),
             vmem((EFF, D), BF16),
+            vmem((8, BLK), jnp.int32),
+            vmem((8, BLK), F32),
             vmem((4, 16, BLK), F32),
             vmem((HEADS, BLK, HEAD), F32),
             vmem((HEADS, BLK, HEAD), F32),
@@ -418,28 +435,28 @@
             vmem((ROWS, D), F32),
             vmem((4, 8 * SLOTS, BLK), BF16),
             vmem((4, BLK, 8 * SLOTS), BF16),
-            vmem((4, BLK, D), BF16),
+            vmem((16, ROWS, D), BF16),
             vmem((4, 8 * SLOTS, D), BF16),
             vmem((4, 8 * SLOTS, D), BF16),
             vmem((4, 8 * SLOTS, D), BF16),
             vmem((4, 8 * SLOTS, D), BF16),
-            vmem((4, BLK, D), F32),
+            vmem((16, ROWS, D), F32),
             vmem((8, ROWS, D), BF16),
             vmem((7, ROWS, D), BF16),
             vmem((8, ROWS, D), BF16),
             vmem((7, ROWS, D), BF16),
             vmem((ROWS, D), BF16),
-            dma((9,)),
-            dma((180,)),
+            dma((10,)),
+            dma((256,)),
             dma((32,)),
             dma((4,)),
-            dma((2, 3)),
-            dma((2, 8)),
-            dma((2, 7)),
+            dma((4, 3)),
+            dma((4, 8)),
+            dma((4, 7)),
             dma((4, 8)),
             dma((4, 8)),
-            dma((2, 8)),
-            dma((2, 7)),
+            dma((4, 8)),
+            dma((4, 7)),
             dma((10,)),
         ],
         compiler_params=pltpu.CompilerParams(
@@ -448,7 +465,8 @@
         name="layer",
     )(
         queries, keys, values, out_weight, norm_gain.reshape(1, D),
-        expert_gate.reshape(D, EFF), expert_up.reshape(D, EFF), expert_down.reshape(EFF, D), route,
+        expert_gate.reshape(D, EFF), expert_up.reshape(D, EFF), expert_down.reshape(EFF, D),
+        expert_ids.T, route_weights.T,
     )
 
 

time: 171 us -> 162 us (0.947)
  Pallas kernels: 165 us -> 158 us
  other arithmetic: 1.98 us -> 0 us
    pallas_call x1, Pallas kernels: 165 us -> 158 us  [per_device(): pl.pallas_call(layer_kernel, out_shape=(jax.ShapeDtypeStruct((BLK, HEADS...]
where the time goes in v2:
time: 162 us
  Pallas kernels  158 us (98%)
  local copies, waits for them, and re-layouts  3.24 us (2%)
    pallas_call x1, Pallas kernels, per_device(): pl.pallas_call(layer_kernel, out_shape=(jax.ShapeDtypeStruct((BLK, HEADS...  158 us

profile of v2, /device:TPU:48, one launch (start us, length us, event | category | flops | bytes accessed | tf_op | source)
XLA Modules:
  0.0 161.6 jit_solution(6277398263623271191)
XLA Ops:
  0.6 157.7 %layer.1 = (bf16[128,1024]{1,0:T(8,128)(2,1)}, bf16[32,2048]{1,0:T(8,128)(2,1)}) custom-call(bf16[128,1024]{1,0:T(8,128)(2,1)} %q_hbm.1, bf16[128,128]{1,0:T(8,128)(2,1)} %k_hbm.1, bf16[128,128]{1,0:T(8,128)(2,1)} %v_hbm.1, bf16[1024,2048]{1,0:T(8,128)(2,1)} %w_hbm.1, f32[1,2048]{1,0:T(1,128)} %bitcast.9, bf16[2048,384]{1,0:T(8,128)(2,1)} %bitcast.6, ...), custom_call_target="tpu_custom_call" | custom-call | tf_op jit(solution)/shard_map/layer/pallas_call | solution.py:408
  158.4 1.7 %copy.14 = bf16[128,1024]{1,0:T(8,128)(2,1)} copy(bf16[128,1024]{1,0:T(8,128)(2,1)} %get-tuple-element.4) | data formatting | bytes 524288
  160.0 1.6 copy.15

commit v3 on v2

--- a/solution.py
+++ b/solution.py
@@ -17,16 +17,18 @@
 EFF = 384
 ROWS = 32
 SLOTS = 16
+CHUNKS = 16
+WIDE = D // CHUNKS
 NEG = -1e30
 
 
 def layer_kernel(
     q_hbm, k_hbm, v_hbm, w_hbm, gain_hbm, gate_hbm, up_hbm, down_hbm, ids_hbm, share_hbm,
-    att_hbm, out_hbm,
+    att_v, out_v,
     q_v, q_h, kv, w_v, gain_v, gate_v, up_v, down_v, ids_v, share_v, route,
-    m_s, l_s, acc_s, att_v, proj_f, rs_s, rs_r, proj_own,
-    dmap, mmap, xg, xs, xr, ys, ret, contrib, sp, sm, rp, rm, out_v,
-    load_sem, send_sem, kv_sem, route_sem, rs_sem, agp_sem, agm_sem, xd_sem, xb_sem, rp_sem, rm_sem, self_sem,
+    m_s, l_s, acc_s, proj_f, rs_s, rs_r, proj_own,
+    dmap, mmap, xg, xs, xr, ys, ret, contrib, sp, sm, rp, rm,
+    load_sem, send_sem, ring_send, kv_sem, kvz_sem, route_sem, rs_sem, agp_sem, agm_sem, xd_sem, xb_sem, rp_sem, rm_sem, self_sem,
 ):
     ctx = lax.axis_index("ctx")
     tp = lax.axis_index("tp")
@@ -114,8 +116,13 @@
     def x_row(dx):
         return ((x + dx) % 4) * 2 + core
 
-    for d in (1, 3):
-        send_block(ctx, at_zh((zh + d) % 4))
+    def half_block(z_hi, half):
+        return kv.at[z_hi * 8 + row, pl.ds(half * BLK, BLK)]
+
+    for half in range(2):
+        for d in (1, 3):
+            here = half_block(zh, half)
+            send(here, here, kvz_sem.at[zh, half], at_zh((zh + d) % 4))
     for dx in (2, 1, 3):
         send_block(ctx, at_row(x_row(dx)))
     send_block(ctx, at_row(sibling))
@@ -181,10 +188,14 @@
             send_block(block, at_row(x_row(dx)))
         send_block(block, at_row(sibling))
 
-    for d in (3, 1):
-        block = ((zh + d) % 4) * 8 + row
-        arrived(kv.at[block], kv_sem.at[block])
-    send_block(((zh + 3 + 2 * core) % 4) * 8 + row, at_zh((zh + 1 + 2 * core) % 4))
+    passed = (zh + 3 + 2 * core) % 4
+    other = (zh + 1 + 2 * core) % 4
+    for half in range(2):
+        here = half_block(passed, half)
+        arrived(here, kvz_sem.at[passed, half])
+        send(here, here, kvz_sem.at[passed, half], at_zh(other))
+    for half in range(2):
+        arrived(half_block(other, half), kvz_sem.at[other, half])
     for d in (3, 1):
         spread(((zh + d) % 4) * 8 + row)
     for d in (3, 1):
@@ -202,9 +213,10 @@
             attend(s, False)
 
     attend_earlier(3)
-    block = ((zh + 2) % 4) * 8 + row
-    arrived(kv.at[block], kv_sem.at[block])
-    spread(block)
+    far = (zh + 2) % 4
+    for half in range(2):
+        arrived(half_block(far, half), kvz_sem.at[far, half])
+    spread(far * 8 + row)
     attend_earlier(1)
 
     src = (zh + 2) % 4
@@ -238,8 +250,6 @@
         att_v[:, h * HEAD : (h + 1) * HEAD] = (
             acc_s[h] / jnp.sum(l_s[h], axis=1, keepdims=True)
         ).astype(BF16)
-    att_store = pltpu.make_async_copy(att_v, att_hbm, self_sem.at[8])
-    att_store.start()
 
     loads["w"].wait()
     for n in range(4):
@@ -266,26 +276,37 @@
     )
     proj_own[...] = projected
     inverse = lax.rsqrt(jnp.mean(projected * projected, axis=1, keepdims=True) + 1e-06)
-    xg[z] = (projected * inverse * gain_v[...]).astype(BF16)
-
-    def piece(origin, n):
-        return xg.at[origin, :, pl.ds(n * 512, 512)]
+    normed = (projected * inverse * gain_v[...]).astype(BF16)
+    for j in range(CHUNKS):
+        xg[z, j] = normed[:, j * WIDE : (j + 1) * WIDE]
+
+    def pass_on(src, dst, sems, send_at, j, k, device):
+        pltpu.make_async_remote_copy(
+            src_ref=src, dst_ref=dst, send_sem=ring_send.at[send_at], recv_sem=sems.at[j, k - 1],
+            device_id=device, device_id_type=MESH,
+        ).start()
 
     def ring_step(k):
-        for n in range(4):
-            here = piece(zmod(1 - k), n)
+        def chunk(j, carry):
+            here = xg.at[zmod(1 - k), j]
             if k > 1:
-                arrived(here, agp_sem.at[n, k - 2])
-            send(here, here, agp_sem.at[n, k - 1], above)
-            here = piece(zmod(k - 1), n)
+                arrived(here, agp_sem.at[j, k - 2])
+            pass_on(here, here, agp_sem, 0, j, k, above)
+            here = xg.at[zmod(k - 1), j]
             if k > 1:
-                arrived(here, agm_sem.at[n, k - 2])
+                arrived(here, agm_sem.at[j, k - 2])
             if k <= 7:
-                send(here, here, agm_sem.at[n, k - 1], below)
+                pass_on(here, here, agm_sem, 0, j, k, below)
+            return carry
+
+        lax.fori_loop(0, CHUNKS, chunk, 0)
 
     def ring_end():
-        for n in range(4):
-            arrived(piece(zmod(-8), n), agp_sem.at[n, 7])
+        def chunk(j, carry):
+            arrived(xg.at[zmod(-8), j], agp_sem.at[j, 7])
+            return carry
+
+        lax.fori_loop(0, CHUNKS, chunk, 0)
 
     side = 2 * (tp // 2) - 1
     order = [zh, (zh + side + 4) % 4, (zh - side + 4) % 4, (zh + 2) % 4]
@@ -313,10 +334,12 @@
     def dispatch(i):
         for n in range(4):
             cols = pl.ds(n * 512, 512)
+            tokens = [
+                xg[pl.ds(order[i] * 4, 4), j].reshape(BLK, WIDE)
+                for j in range(n * 512 // WIDE, (n + 1) * 512 // WIDE)
+            ]
             xs[i, :, cols] = jnp.dot(
-                dmap[order[i]],
-                xg[pl.ds(order[i] * 4, 4), :, cols].reshape(BLK, 512),
-                preferred_element_type=F32,
+                dmap[order[i]], jnp.concatenate(tokens, axis=1), preferred_element_type=F32
             ).astype(BF16)
         exchange(xs, xr, xd_sem, i, i)
 
@@ -337,9 +360,11 @@
         exchanged(ret, xb_sem, i, local[4 + i])
         for n in range(4):
             cols = pl.ds(n * 512, 512)
-            contrib[pl.ds(order[i] * 4, 4), :, cols] = jnp.dot(
-                mmap[order[i]], ret[i, :, cols], preferred_element_type=F32
-            ).reshape(4, ROWS, 512)
+            mixed = jnp.dot(mmap[order[i]], ret[i, :, cols], preferred_element_type=F32)
+            for j in range(512 // WIDE):
+                contrib[pl.ds(order[i] * 4, 4), n * 512 // WIDE + j] = mixed[
+                    :, j * WIDE : (j + 1) * WIDE
+                ].reshape(4, ROWS, WIDE)
 
     for k in (1, 2, 3, 4):
         ring_step(k)
@@ -364,45 +389,51 @@
     mix(2)
     mix(3)
 
+    def scatter_step(k):
+        def chunk(j, carry):
+            total = contrib[zmod(9 - k), j]
+            if k > 1:
+                arrived(rp.at[k - 2, j], rp_sem.at[j, k - 2])
+                total = total + rp[k - 2, j].astype(F32)
+            sp[k - 1, j] = total.astype(BF16)
+            pass_on(sp.at[k - 1, j], rp.at[k - 1, j], rp_sem, 1, j, k, above)
+            if k <= 7:
+                total = contrib[zmod(k - 8), j]
+                if k > 1:
+                    arrived(rm.at[k - 2, j], rm_sem.at[j, k - 2])
+                    total = total + rm[k - 2, j].astype(F32)
+                sm[k - 1, j] = total.astype(BF16)
+                pass_on(sm.at[k - 1, j], rm.at[k - 1, j], rm_sem, 2, j, k, below)
+            return carry
+
+        lax.fori_loop(0, CHUNKS, chunk, 0)
+
     for k in range(1, 9):
-        for n in range(4):
-            cols = pl.ds(n * 512, 512)
-            total = contrib[zmod(9 - k), :, cols]
-            if k > 1:
-                arrived(rp.at[k - 2, :, cols], rp_sem.at[n, k - 2])
-                total = total + rp[k - 2, :, cols].astype(F32)
-            sp[k - 1, :, cols] = total.astype(BF16)
-            send(sp.at[k - 1, :, cols], rp.at[k - 1, :, cols], rp_sem.at[n, k - 1], above)
-            if k <= 7:
-                total = contrib[zmod(k - 8), :, cols]
-                if k > 1:
-                    arrived(rm.at[k - 2, :, cols], rm_sem.at[n, k - 2])
-                    total = total + rm[k - 2, :, cols].astype(F32)
-                sm[k - 1, :, cols] = total.astype(BF16)
-                send(sm.at[k - 1, :, cols], rm.at[k - 1, :, cols], rm_sem.at[n, k - 1], below)
-    for n in range(4):
-        cols = pl.ds(n * 512, 512)
-        arrived(rm.at[6, :, cols], rm_sem.at[n, 6])
-        arrived(rp.at[7, :, cols], rp_sem.at[n, 7])
+        scatter_step(k)
+    for j in range(CHUNKS):
+        cols = pl.ds(j * WIDE, WIDE)
+        arrived(rm.at[6, j], rm_sem.at[j, 6])
+        arrived(rp.at[7, j], rp_sem.at[j, 7])
         out_v[:, cols] = (
             proj_own[:, cols]
-            + contrib[z, :, cols]
-            + rp[7, :, cols].astype(F32)
-            + rm[6, :, cols].astype(F32)
+            + contrib[z, j]
+            + rp[7, j].astype(F32)
+            + rm[6, j].astype(F32)
         ).astype(BF16)
-    out_store = pltpu.make_async_copy(out_v, out_hbm, self_sem.at[9])
-    out_store.start()
+    for i, sent in enumerate((xg.at[pl.ds(0, 15)], sp, sm)):
+        pltpu.make_async_remote_copy(
+            src_ref=sent, dst_ref=sent, send_sem=ring_send.at[i], recv_sem=ring_send.at[i],
+            device_id=above, device_id_type=MESH,
+        ).wait_send()
     for copy in sends:
         copy.wait_send()
-    att_store.wait()
-    out_store.wait()
 
 
 def per_device(
     queries, keys, values, out_weight, norm_gain,
     expert_gate, expert_up, expert_down, expert_ids, route_weights,
 ):
-    any_spec = pl.BlockSpec(memory_space=pl.ANY)
+    hbm_spec = pl.BlockSpec(memory_space=pl.ANY)
     vmem = pltpu.VMEM
     dma = pltpu.SemaphoreType.DMA
     return pl.pallas_call(
@@ -411,8 +442,8 @@
             jax.ShapeDtypeStruct((BLK, HEADS * HEAD), BF16),
             jax.ShapeDtypeStruct((ROWS, D), BF16),
         ),
-        in_specs=[any_spec] * 10,
-        out_specs=(any_spec, any_spec),
+        in_specs=[hbm_spec] * 10,
+        out_specs=(pl.BlockSpec(memory_space=vmem), pl.BlockSpec(memory_space=vmem)),
         scratch_shapes=[
             vmem((BLK, HEADS * HEAD), BF16),
             vmem((HEADS, BLK, HEAD), BF16),
@@ -428,39 +459,39 @@
             vmem((HEADS, BLK, HEAD), F32),
             vmem((HEADS, BLK, HEAD), F32),
             vmem((HEADS, BLK, HEAD), F32),
-            vmem((BLK, HEADS * HEAD), BF16),
             vmem((BLK, D), F32),
             vmem((BLK, D), BF16),
             vmem((3, ROWS, D), BF16),
             vmem((ROWS, D), F32),
             vmem((4, 8 * SLOTS, BLK), BF16),
             vmem((4, BLK, 8 * SLOTS), BF16),
-            vmem((16, ROWS, D), BF16),
+            vmem((16, CHUNKS, ROWS, WIDE), BF16),
             vmem((4, 8 * SLOTS, D), BF16),
             vmem((4, 8 * SLOTS, D), BF16),
             vmem((4, 8 * SLOTS, D), BF16),
             vmem((4, 8 * SLOTS, D), BF16),
-            vmem((16, ROWS, D), F32),
-            vmem((8, ROWS, D), BF16),
-            vmem((7, ROWS, D), BF16),
-            vmem((8, ROWS, D), BF16),
-            vmem((7, ROWS, D), BF16),
-            vmem((ROWS, D), BF16),
+            vmem((16, CHUNKS, ROWS, WIDE), F32),
+            vmem((8, CHUNKS, ROWS, WIDE), BF16),
+            vmem((7, CHUNKS, ROWS, WIDE), BF16),
+            vmem((8, CHUNKS, ROWS, WIDE), BF16),
+            vmem((7, CHUNKS, ROWS, WIDE), BF16),
             dma((10,)),
-            dma((256,)),
+            dma((128,)),
+            dma((3,)),
             dma((32,)),
+            dma((4, 2)),
             dma((4,)),
             dma((4, 3)),
-            dma((4, 8)),
-            dma((4, 7)),
+            dma((CHUNKS, 8)),
+            dma((CHUNKS, 7)),
             dma((4, 8)),
             dma((4, 8)),
-            dma((4, 8)),
-            dma((4, 7)),
-            dma((10,)),
+            dma((CHUNKS, 8)),
+            dma((CHUNKS, 7)),
+            dma((8,)),
         ],
         compiler_params=pltpu.CompilerParams(
-            collective_id=0, has_side_effects=True, vmem_limit_bytes=60 * 1024 * 1024
+            collective_id=0, has_side_effects=True, vmem_limit_bytes=53 * 1024 * 1024
         ),
         name="layer",
     )(

time: 162 us -> 164 us (1.012)
  local copies, waits for them, and re-layouts: 3.24 us -> 5.89 us
    unnamed x2 -> x14, local copies, waits for them, and re-layouts: 3.24 us -> 5.89 us
where the time goes in v3:
time: 164 us
  Pallas kernels  157 us (96%)
  local copies, waits for them, and re-layouts  5.89 us (4%)
    pallas_call x1, Pallas kernels, per_device(): pl.pallas_call(layer_kernel, out_shape=(jax.ShapeDtypeStruct((BLK, HEADS...  157 us
    unnamed x14, local copies, waits for them, and re-layouts  5.89 us

profile of v3, /device:TPU:48, one launch (start us, length us, event | category | flops | bytes accessed | tf_op | source)
XLA Modules:
  0.0 163.7 jit_solution(12351256118669917978)
XLA Ops:
  0.6 0.0 copy-start
  0.6 0.9 copy-done
  1.6 0.0 copy-start.1
  1.6 0.8 copy-done.1
  2.3 0.0 copy-start.2
  2.3 0.8 copy-done.2
  3.1 0.0 copy-start.3
  3.1 0.7 copy-done.3
  3.8 0.0 copy-start.4
  3.8 0.7 copy-done.4
  4.5 0.0 copy-start.5
  4.5 0.7 copy-done.5
  5.2 157.1 %layer.1 = (bf16[128,1024]{1,0:T(8,128)(2,1)S(1)}, bf16[32,2048]{1,0:T(8,128)(2,1)S(1)}) custom-call(bf16[128,1024]{1,0:T(8,128)(2,1)S(1)} %copy-done, bf16[128,128]{1,0:T(8,128)(2,1)S(1)} %copy-done.1, bf16[128,128]{1,0:T(8,128)(2,1)S(1)} %copy-done.2, bf16[1024,2048]{1,0:T(8,128)(2,1)} %w_hbm.1, f32[1,2048]{1,0:T(1,128)S(1)} %bitcast.6, ...), custom_call_target="tpu_custom_call" | custom-call | tf_op jit(solution)/shard_map/layer/pallas_call | solution.py:439
  162.3 0.7 copy.14
  163.0 0.7 copy.15
Async XLA Ops:
  0.6 1.0 copy-start
  1.6 0.8 copy-start.1
  2.3 0.8 copy-start.2
  3.1 0.7 copy-start.3
  3.8 0.7 copy-start.4
  4.5 0.7 copy-start.5

commit v4 on v3

--- a/solution.py
+++ b/solution.py
@@ -169,7 +169,7 @@
             m_s[h] = new_max
             return carry
 
-        lax.fori_loop(0, HEADS, head, 0)
+        lax.fori_loop(0, HEADS, head, 0, unroll=2)
 
     def collect(s):
         for dx in (1, 3, 2):
@@ -436,6 +436,14 @@
     hbm_spec = pl.BlockSpec(memory_space=pl.ANY)
     vmem = pltpu.VMEM
     dma = pltpu.SemaphoreType.DMA
+    pinned = [
+        pltpu.with_memory_space_constraint(operand, pltpu.HBM)
+        for operand in (
+            queries, keys, values, out_weight, norm_gain.reshape(1, D),
+            expert_gate.reshape(D, EFF), expert_up.reshape(D, EFF), expert_down.reshape(EFF, D),
+            expert_ids.T, route_weights.T,
+        )
+    ]
     return pl.pallas_call(
         layer_kernel,
         out_shape=(
@@ -494,11 +502,7 @@
             collective_id=0, has_side_effects=True, vmem_limit_bytes=53 * 1024 * 1024
         ),
         name="layer",
-    )(
-        queries, keys, values, out_weight, norm_gain.reshape(1, D),
-        expert_gate.reshape(D, EFF), expert_up.reshape(D, EFF), expert_down.reshape(EFF, D),
-        expert_ids.T, route_weights.T,
-    )
+    )(*pinned)
 
 
 def solution(mesh):

time: 164 us -> 157 us (0.957)
  the two profiles are of different devices: /device:TPU:48 before, /device:TPU:40 now
where the time goes in v4:
time: 157 us
  Pallas kernels  155 us (99%)
    pallas_call x1, Pallas kernels, per_device(): pl.pallas_call(layer_kernel, out_shape=(jax.ShapeDtypeStruct((BLK, HEADS...  155 us

profile of v4, /device:TPU:40, one launch (start us, length us, event | category | flops | bytes accessed | tf_op | source)
XLA Modules:
  0.0 157.0 jit_solution(4059345392245737530)
XLA Ops:
  0.6 155.0 %layer.1 = (bf16[128,1024]{1,0:T(8,128)(2,1)S(1)}, bf16[32,2048]{1,0:T(8,128)(2,1)S(1)}) custom-call(bf16[128,1024]{1,0:T(8,128)(2,1)} %q_hbm.1, bf16[128,128]{1,0:T(8,128)(2,1)} %k_hbm.1, bf16[128,128]{1,0:T(8,128)(2,1)} %v_hbm.1, bf16[1024,2048]{1,0:T(8,128)(2,1)} %w_hbm.1, f32[1,2048]{1,0:T(1,128)} %bitcast.9, bf16[2048,384]{1,0:T(8,128)(2,1)} %bitcast.6, ...), custom_call_target="tpu_custom_call" | custom-call | tf_op jit(solution)/shard_map/layer/pallas_call | solution.py:447
  155.6 0.7 copy.14
  156.3 0.7 copy.15

commit v5 on v4

--- a/solution.py
+++ b/solution.py
@@ -169,7 +169,7 @@
             m_s[h] = new_max
             return carry
 
-        lax.fori_loop(0, HEADS, head, 0, unroll=2)
+        lax.fori_loop(0, HEADS, head, 0, unroll=4)
 
     def collect(s):
         for dx in (1, 3, 2):
@@ -219,6 +219,27 @@
     spread(far * 8 + row)
     attend_earlier(1)
 
+    attend_earlier(2)
+
+    for h in range(HEADS):
+        att_v[:, h * HEAD : (h + 1) * HEAD] = (
+            acc_s[h] / jnp.sum(l_s[h], axis=1, keepdims=True)
+        ).astype(BF16)
+
+    loads["w"].wait()
+    for n in range(4):
+        cols = pl.ds(n * 512, 512)
+        part = jnp.dot(att_v[...], w_v[:, cols], preferred_element_type=F32)
+        proj_f[:, cols] = part
+        rs_s[:, cols] = part.astype(BF16)
+        for o in (2, 1, 3):
+            owner = (tp + o) % 4
+            send(
+                rs_s.at[pl.ds(pl.multiple_of(owner * ROWS, ROWS), ROWS), cols],
+                rs_r.at[o - 1, :, cols],
+                rs_sem.at[n, o - 1],
+                at_tp(owner),
+            )
     src = (zh + 2) % 4
     arrived(route.at[src], route_sem.at[src])
     earlier = (
@@ -244,27 +265,6 @@
         back = jnp.concatenate([choose[r] * picked[r] for r in range(8)], axis=0)
         mmap[b] = back.T.astype(BF16)
 
-    attend_earlier(2)
-
-    for h in range(HEADS):
-        att_v[:, h * HEAD : (h + 1) * HEAD] = (
-            acc_s[h] / jnp.sum(l_s[h], axis=1, keepdims=True)
-        ).astype(BF16)
-
-    loads["w"].wait()
-    for n in range(4):
-        cols = pl.ds(n * 512, 512)
-        part = jnp.dot(att_v[...], w_v[:, cols], preferred_element_type=F32)
-        proj_f[:, cols] = part
-        rs_s[:, cols] = part.astype(BF16)
-        for o in (2, 1, 3):
-            owner = (tp + o) % 4
-            send(
-                rs_s.at[pl.ds(pl.multiple_of(owner * ROWS, ROWS), ROWS), cols],
-                rs_r.at[o - 1, :, cols],
-                rs_sem.at[n, o - 1],
-                at_tp(owner),
-            )
     loads["gain"].wait()
     for n in range(4):
         cols = pl.ds(n * 512, 512)

time: 157 us -> 156 us (level)
  the two profiles are of different devices: /device:TPU:40 before, /device:TPU:48 now
where the time goes in v5:
time: 156 us
  Pallas kernels  154 us (99%)
    pallas_call x1, Pallas kernels, per_device(): pl.pallas_call(layer_kernel, out_shape=(jax.ShapeDtypeStruct((BLK, HEADS...  154 us

profile of v5, /device:TPU:48, one launch (start us, length us, event | category | flops | bytes accessed | tf_op | source)
XLA Modules:
  0.0 155.6 jit_solution(3690169661312720875)
XLA Ops:
  0.6 153.6 %layer.1 = (bf16[128,1024]{1,0:T(8,128)(2,1)S(1)}, bf16[32,2048]{1,0:T(8,128)(2,1)S(1)}) custom-call(bf16[128,1024]{1,0:T(8,128)(2,1)} %q_hbm.1, bf16[128,128]{1,0:T(8,128)(2,1)} %k_hbm.1, bf16[128,128]{1,0:T(8,128)(2,1)} %v_hbm.1, bf16[1024,2048]{1,0:T(8,128)(2,1)} %w_hbm.1, f32[1,2048]{1,0:T(1,128)} %bitcast.9, bf16[2048,384]{1,0:T(8,128)(2,1)} %bitcast.6, ...), custom_call_target="tpu_custom_call" | custom-call | tf_op jit(solution)/shard_map/layer/pallas_call | solution.py:447
  154.2 0.7 copy.14
  154.9 0.7 copy.15
